TPU v7x, 512 devices: a whole 4x4x16 slice. The times are simulated.
512 devices in a mesh: gx: 16 (over z), gz: 8 (over y_lo, x), pa: 4 (over y_hi, core).
Axes of the slice: x: 4, y: 4 (y_hi: 2, y_lo: 2; y = y_hi * 2 + y_lo), z: 16, core: 2. Of those that a mesh axis runs over, the one named last changes fastest.
Arguments:
- velocity: float32 [8, 128, 128, 512], P('pa', 'gx', 'gz'), may hold values from 0.7 to 2.3
- wave_now: float32 [8, 128, 128, 512], P('pa', 'gx', 'gz'), may hold values from -6 to 6
- wave_prev: float32 [8, 128, 128, 512], P('pa', 'gx', 'gz'), may hold values from -6 to 6
- observed: float32 [128, 128, 512], P('gx', 'gz'), may hold values from -6 to 6
- receiver: int32 [128, 128, 512], P('gx', 'gz'), may hold values 0 or 1
- spread: int32 [2], replicated, may hold values from 100 to 10000, as said below
Outputs:
- update: float32 [8, 128, 128, 512], P('pa', 'gx', 'gz')
Inputs may be any that keep to these rules, and one draw needn't show every extreme that they name: spread[0] is the numerator, 100 to 200, and spread[1] the denominator, 10000.
All inputs are finite; a program needn't handle non-finite values. No bound on the sum of `receiver` on one device may be relied on, other than what follows from the above.
Results may differ from a plain program's by a relative error of at most 0.0003.
Values sent between devices are 32-bit elements; how exact they have to be, the bound alone decides.
A program may use at most 64 MiB of HBM per device.

v0:
```python
import jax
import jax.numpy as jnp
from jax import lax
from jax.sharding import PartitionSpec as P

STEPS = 4


courant = 0.045
centre_coef = -7.5
near_coef = 4.0 / 3.0
far_coef = -1.0 / 12.0


def padded_2(block, sides, width):
    for axis, dim in sides:
        count = lax.axis_size(axis)
        forward = [(i, i + 1) for i in range(count - 1)]
        backward = [(target, source) for source, target in forward]
        low = lax.ppermute(
            lax.slice_in_dim(block, block.shape[dim] - width, None, axis=dim), axis, forward
        )
        high = lax.ppermute(lax.slice_in_dim(block, 0, width, axis=dim), axis, backward)
        block = jnp.concatenate([low, block, high], axis=dim)
    return block


def shifted(padded, which_dim, offset, dims):
    starts = [0, 2, 2, 2]
    starts[which_dim] += offset
    limits = [starts[k] + dims[k] for k in range(4)]
    return lax.slice(padded, starts, limits)


def laplace(wave_field):
    dims = wave_field.shape
    padded = padded_2(wave_field, (("gx", 1), ("gz", 2)), 2)
    padded = jnp.pad(padded, ((0, 0), (0, 0), (0, 0), (2, 2)))
    summed = centre_coef * wave_field
    for which_dim in range(1, 4):
        summed = summed + near_coef * (
            shifted(padded, which_dim, -1, dims) + shifted(padded, which_dim, 1, dims)
        )
        summed = summed + far_coef * (
            shifted(padded, which_dim, -2, dims) + shifted(padded, which_dim, 2, dims)
        )
    return summed


def pair_sums(mine, everyone):
    differences = mine[:, None] - everyone[None]
    return jnp.sum(differences * differences, axis=(2, 3, 4))


def wave_gradient(velocity, wave_now, wave_prev, observed, receiver):
    coefficient = courant * velocity * velocity
    previous, current = (wave_prev, wave_now)
    laplacians = []
    for step_index in range(STEPS):
        applied = laplace(current)
        laplacians.append(applied)
        previous, current = (current, 2.0 * current - previous + coefficient * applied)
    receiver_mask = receiver.astype(jnp.float32)
    adjoint_next = receiver_mask[None] * (current - observed[None])
    lagging = jnp.zeros_like(adjoint_next)
    summed = jnp.zeros_like(adjoint_next)
    for step_index in reversed(range(STEPS)):
        summed = summed + adjoint_next * laplacians[step_index]
        if step_index > 0:
            earlier = 2.0 * adjoint_next - lagging + laplace(coefficient * adjoint_next)
            lagging, adjoint_next = (adjoint_next, earlier)
    return 2.0 * courant * velocity * summed


def local(velocity, wave_now, wave_prev, observed, receiver, spread):
    width_scale = spread[0].astype(jnp.float32) / spread[1].astype(jnp.float32)
    cell_count = (
        velocity.shape[1]
        * lax.axis_size("gx")
        * velocity.shape[2]
        * lax.axis_size("gz")
        * velocity.shape[3]
    )
    count = velocity.shape[0] * lax.axis_size("pa")
    gradient = wave_gradient(velocity, wave_now, wave_prev, observed, receiver)
    everyone, gradient_all = (
        lax.all_gather(velocity, "pa", axis=0, tiled=True),
        lax.all_gather(gradient, "pa", axis=0, tiled=True),
    )
    summed = lax.psum(pair_sums(velocity, everyone), ("gx", "gz"))
    weight = jnp.exp(-(summed / cell_count) / width_scale)
    contrib = -gradient_all[None] + 2.0 / width_scale * (velocity[:, None] - everyone[None])
    return jnp.sum(weight[:, :, None, None, None] * contrib, axis=1) / count


def solution(mesh):
    in_specs = (
        P("pa", "gx", "gz", None),
        P("pa", "gx", "gz", None),
        P("pa", "gx", "gz", None),
        P("gx", "gz", None),
        P("gx", "gz", None),
        P(),
    )
    out_specs = P("pa", "gx", "gz", None)
    return jax.shard_map(local, mesh=mesh, in_specs=in_specs, out_specs=out_specs, check_vma=False)
```

profile of v0, /device:TPU:16, one launch (start us, length us, event | category | flops | bytes accessed | tf_op | source)
XLA Modules:
  0.0 498.6 jit_solution(6083300640079504033)
XLA Ops:
  24.3 4.3 collective-permute-done.3
  37.4 5.5 %collective-permute-done.5 = f32[2,2,16,512]{3,2,1,0:T(8,128)S(1)} collective-permute-done((f32[2,2,16,512]{3,2,1,0:T(8,128)S(1)}, f32[2,2,16,512]{3,2,1,0:T(8,128)S(1)}, u32[]{:S(2)}, u32[]{:S(2)}) %collective-permute-start.5) | collective-permute-done | bytes 131104 | tf_op jit(solution)/shard_map/ppermute | solution.py:23
  48.6 4.3 collective-permute-done.7
  54.6 4.9 collective-permute-start.8
  61.9 4.4 collective-permute-done.9
  66.4 4.4 collective-permute-start.10
  73.0 4.3 collective-permute-done.11
  79.0 4.1 collective-permute-start.12
  85.6 4.4 collective-permute-done.13
  90.1 4.0 collective-permute-start.14
  96.3 4.5 collective-permute-done.15
  102.5 4.9 collective-permute-start.16
  109.9 4.4 collective-permute-done.17
  115.0 4.0 collective-permute-start.18
  121.6 4.5 collective-permute-done.19
  129.5 4.9 collective-permute-start.20
  136.9 4.4 collective-permute-done.21
  141.3 4.0 collective-permute-start.22
  147.5 4.3 collective-permute-done.23
  153.5 3.9 collective-permute-start.24
  160.0 4.4 collective-permute-done.25
  164.4 4.2 collective-permute-start.26
  170.8 4.3 collective-permute-done.27
  182.1 305.8 %psum.7 = f32[2,8]{1,0:T(2,128)S(1)} all-reduce(f32[2,8]{1,0:T(2,128)S(1)} %fusion), channel_id=1, replica_groups=mesh['gx'=16,'gz'=8,'pa'=4] {'gx','gz'}, use_global_device_ids=true, to_apply=%region_1.2 | all-reduce | flops 16 | bytes 128 | tf_op jit(solution)/shard_map/psum | solution.py:90
  (95 shorter events, 76.3 us)
Async XLA Ops:
  6.5 173.4 %all-gather.3.cloned.1.call-start = ((), (), s32[]{:S(2)}) async-start(), calls=%async_computation | async-start | bytes 2621440 | tf_op jit(solution)/shard_map/all_gather | solution.py:87
  7.5 6.6 %collective-permute-start = (f32[2,2,16,512]{3,2,1,0:T(8,128)S(1)}, f32[2,2,16,512]{3,2,1,0:T(8,128)S(1)}, u32[]{:S(2)}, u32[]{:S(2)}) collective-permute-start(f32[2,2,16,512]{3,2,1,0:T(8,128)S(1)} %get-tuple-element.48), channel_id=1, source_target_pairs={{0,32},{32,64},{64,96},{96,128},{128,160},{160,192},{192,224},{224... | collective-permute-start | bytes 393224 | tf_op jit(solution)/shard_map/ppermute | solution.py:20
  11.4 7.0 %collective-permute-start.1 = (f32[2,2,16,512]{3,2,1,0:T(8,128)S(1)}, f32[2,2,16,512]{3,2,1,0:T(8,128)S(1)}, u32[]{:S(2)}, u32[]{:S(2)}) collective-permute-start(f32[2,2,16,512]{3,2,1,0:T(8,128)S(1)} %get-tuple-element.47), channel_id=1, source_target_pairs={{32,0},{64,32},{96,64},{128,96},{160,128},{192,160},{224,192},{256... | collective-permute-start | bytes 393224 | tf_op jit(solution)/shard_map/ppermute | solution.py:23
  22.1 6.5 %collective-permute-start.3 = (f32[2,12,2,512]{3,2,1,0:T(2,128)S(1)}, f32[2,12,2,512]{3,2,1,0:T(2,128)S(1)}, u32[]{:S(2)}, u32[]{:S(2)}) collective-permute-start(f32[2,12,2,512]{3,2,1,0:T(2,128)S(1)} %get-tuple-element.31), channel_id=1, source_target_pairs={{4,0},{8,4},{12,8},{16,12},{20,16},{24,20},{28,24},{5,1},{9,5},{13... | collective-permute-start | bytes 294920 | tf_op jit(solution)/shard_map/ppermute | solution.py:23
  34.9 8.0 %collective-permute-start.5 = (f32[2,2,16,512]{3,2,1,0:T(8,128)S(1)}, f32[2,2,16,512]{3,2,1,0:T(8,128)S(1)}, u32[]{:S(2)}, u32[]{:S(2)}) collective-permute-start(f32[2,2,16,512]{3,2,1,0:T(8,128)S(1)} %get-tuple-element.43), channel_id=1, source_target_pairs={{32,0},{64,32},{96,64},{128,96},{160,128},{192,160},{224,192},{256... | collective-permute-start | bytes 393224 | tf_op jit(solution)/shard_map/ppermute | solution.py:23
  46.4 6.5 %collective-permute-start.7 = (f32[2,12,2,512]{3,2,1,0:T(2,128)S(1)}, f32[2,12,2,512]{3,2,1,0:T(2,128)S(1)}, u32[]{:S(2)}, u32[]{:S(2)}) collective-permute-start(f32[2,12,2,512]{3,2,1,0:T(2,128)S(1)} %get-tuple-element.29), channel_id=1, source_target_pairs={{4,0},{8,4},{12,8},{16,12},{20,16},{24,20},{28,24},{5,1},{9,5},{13... | collective-permute-start | bytes 294920 | tf_op jit(solution)/shard_map/ppermute | solution.py:23
  54.6 7.4 %collective-permute-start.8 = (f32[2,2,16,512]{3,2,1,0:T(8,128)S(1)}, f32[2,2,16,512]{3,2,1,0:T(8,128)S(1)}, u32[]{:S(2)}, u32[]{:S(2)}) collective-permute-start(f32[2,2,16,512]{3,2,1,0:T(8,128)S(1)} %get-tuple-element.40), channel_id=1, source_target_pairs={{0,32},{32,64},{64,96},{96,128},{128,160},{160,192},{192,224},{224... | collective-permute-start | bytes 393224 | tf_op jit(solution)/shard_map/ppermute | solution.py:20
  59.4 6.9 %collective-permute-start.9 = (f32[2,2,16,512]{3,2,1,0:T(8,128)S(1)}, f32[2,2,16,512]{3,2,1,0:T(8,128)S(1)}, u32[]{:S(2)}, u32[]{:S(2)}) collective-permute-start(f32[2,2,16,512]{3,2,1,0:T(8,128)S(1)} %get-tuple-element.41), channel_id=1, source_target_pairs={{32,0},{64,32},{96,64},{128,96},{160,128},{192,160},{224,192},{256... | collective-permute-start | bytes 393224 | tf_op jit(solution)/shard_map/ppermute | solution.py:23
  66.4 6.6 %collective-permute-start.10 = (f32[2,12,2,512]{3,2,1,0:T(2,128)S(1)}, f32[2,12,2,512]{3,2,1,0:T(2,128)S(1)}, u32[]{:S(2)}, u32[]{:S(2)}) collective-permute-start(f32[2,12,2,512]{3,2,1,0:T(2,128)S(1)} %get-tuple-element.26), channel_id=1, source_target_pairs={{0,4},{4,8},{8,12},{12,16},{16,20},{20,24},{24,28},{1,5},{5,9},{9,... | collective-permute-start | bytes 294920 | tf_op jit(solution)/shard_map/ppermute | solution.py:20
  70.8 6.5 %collective-permute-start.11 = (f32[2,12,2,512]{3,2,1,0:T(2,128)S(1)}, f32[2,12,2,512]{3,2,1,0:T(2,128)S(1)}, u32[]{:S(2)}, u32[]{:S(2)}) collective-permute-start(f32[2,12,2,512]{3,2,1,0:T(2,128)S(1)} %get-tuple-element.27), channel_id=1, source_target_pairs={{4,0},{8,4},{12,8},{16,12},{20,16},{24,20},{28,24},{5,1},{9,5},{13... | collective-permute-start | bytes 294920 | tf_op jit(solution)/shard_map/ppermute | solution.py:23
  79.0 6.6 %collective-permute-start.12 = (f32[2,2,16,512]{3,2,1,0:T(8,128)S(1)}, f32[2,2,16,512]{3,2,1,0:T(8,128)S(1)}, u32[]{:S(2)}, u32[]{:S(2)}) collective-permute-start(f32[2,2,16,512]{3,2,1,0:T(8,128)S(1)} %get-tuple-element.38), channel_id=1, source_target_pairs={{0,32},{32,64},{64,96},{96,128},{128,160},{160,192},{192,224},{224... | collective-permute-start | bytes 393224 | tf_op jit(solution)/shard_map/ppermute | solution.py:20
  83.1 6.9 %collective-permute-start.13 = (f32[2,2,16,512]{3,2,1,0:T(8,128)S(1)}, f32[2,2,16,512]{3,2,1,0:T(8,128)S(1)}, u32[]{:S(2)}, u32[]{:S(2)}) collective-permute-start(f32[2,2,16,512]{3,2,1,0:T(8,128)S(1)} %get-tuple-element.39), channel_id=1, source_target_pairs={{32,0},{64,32},{96,64},{128,96},{160,128},{192,160},{224,192},{256... | collective-permute-start | bytes 393224 | tf_op jit(solution)/shard_map/ppermute | solution.py:23
  94.1 6.6 %collective-permute-start.15 = (f32[2,12,2,512]{3,2,1,0:T(2,128)S(1)}, f32[2,12,2,512]{3,2,1,0:T(2,128)S(1)}, u32[]{:S(2)}, u32[]{:S(2)}) collective-permute-start(f32[2,12,2,512]{3,2,1,0:T(2,128)S(1)} %get-tuple-element.25), channel_id=1, source_target_pairs={{4,0},{8,4},{12,8},{16,12},{20,16},{24,20},{28,24},{5,1},{9,5},{13... | collective-permute-start | bytes 294920 | tf_op jit(solution)/shard_map/ppermute | solution.py:23
  102.5 7.4 %collective-permute-start.16 = (f32[2,2,16,512]{3,2,1,0:T(8,128)S(1)}, f32[2,2,16,512]{3,2,1,0:T(8,128)S(1)}, u32[]{:S(2)}, u32[]{:S(2)}) collective-permute-start(f32[2,2,16,512]{3,2,1,0:T(8,128)S(1)} %get-tuple-element.36), channel_id=1, source_target_pairs={{0,32},{32,64},{64,96},{96,128},{128,160},{160,192},{192,224},{224... | collective-permute-start | bytes 393224 | tf_op jit(solution)/shard_map/ppermute | solution.py:20
  107.4 6.9 %collective-permute-start.17 = (f32[2,2,16,512]{3,2,1,0:T(8,128)S(1)}, f32[2,2,16,512]{3,2,1,0:T(8,128)S(1)}, u32[]{:S(2)}, u32[]{:S(2)}) collective-permute-start(f32[2,2,16,512]{3,2,1,0:T(8,128)S(1)} %get-tuple-element.37), channel_id=1, source_target_pairs={{32,0},{64,32},{96,64},{128,96},{160,128},{192,160},{224,192},{256... | collective-permute-start | bytes 393224 | tf_op jit(solution)/shard_map/ppermute | solution.py:23
  115.0 6.5 %collective-permute-start.18 = (f32[2,12,2,512]{3,2,1,0:T(2,128)}, f32[2,12,2,512]{3,2,1,0:T(2,128)S(1)}, u32[]{:S(2)}, u32[]{:S(2)}) collective-permute-start(f32[2,12,2,512]{3,2,1,0:T(2,128)} %get-tuple-element.22), channel_id=1, source_target_pairs={{0,4},{4,8},{8,12},{12,16},{16,20},{20,24},{24,28},{1,5},{5,9},{9,... | collective-permute-start | bytes 294920 | tf_op jit(solution)/shard_map/ppermute | solution.py:20
  119.1 7.0 %collective-permute-start.19 = (f32[2,12,2,512]{3,2,1,0:T(2,128)}, f32[2,12,2,512]{3,2,1,0:T(2,128)}, u32[]{:S(2)}, u32[]{:S(2)}) collective-permute-start(f32[2,12,2,512]{3,2,1,0:T(2,128)} %get-tuple-element.23), channel_id=1, source_target_pairs={{4,0},{8,4},{12,8},{16,12},{20,16},{24,20},{28,24},{5,1},{9,5},{13... | collective-permute-start | bytes 294920 | tf_op jit(solution)/shard_map/ppermute | solution.py:23
  120.5 367.4 %all-gather.5.cloned.1.call-start = ((), (), s32[]{:S(2)}) async-start(), calls=%async_computation.1 | async-start | bytes 2621440 | tf_op jit(solution)/shard_map/all_gather | solution.py:88
  129.5 7.4 %collective-permute-start.20 = (f32[2,2,16,512]{3,2,1,0:T(8,128)S(1)}, f32[2,2,16,512]{3,2,1,0:T(8,128)S(1)}, u32[]{:S(2)}, u32[]{:S(2)}) collective-permute-start(f32[2,2,16,512]{3,2,1,0:T(8,128)S(1)} %get-tuple-element.34), channel_id=1, source_target_pairs={{0,32},{32,64},{64,96},{96,128},{128,160},{160,192},{192,224},{224... | collective-permute-start | bytes 393224 | tf_op jit(solution)/shard_map/ppermute | solution.py:20
  134.4 6.9 %collective-permute-start.21 = (f32[2,2,16,512]{3,2,1,0:T(8,128)S(1)}, f32[2,2,16,512]{3,2,1,0:T(8,128)S(1)}, u32[]{:S(2)}, u32[]{:S(2)}) collective-permute-start(f32[2,2,16,512]{3,2,1,0:T(8,128)S(1)} %get-tuple-element.35), channel_id=1, source_target_pairs={{32,0},{64,32},{96,64},{128,96},{160,128},{192,160},{224,192},{256... | collective-permute-start | bytes 393224 | tf_op jit(solution)/shard_map/ppermute | solution.py:23
  145.4 6.5 %collective-permute-start.23 = (f32[2,12,2,512]{3,2,1,0:T(2,128)S(1)}, f32[2,12,2,512]{3,2,1,0:T(2,128)S(1)}, u32[]{:S(2)}, u32[]{:S(2)}) collective-permute-start(f32[2,12,2,512]{3,2,1,0:T(2,128)S(1)} %get-tuple-element.21), channel_id=1, source_target_pairs={{4,0},{8,4},{12,8},{16,12},{20,16},{24,20},{28,24},{5,1},{9,5},{13... | collective-permute-start | bytes 294920 | tf_op jit(solution)/shard_map/ppermute | solution.py:23
  153.5 6.4 %collective-permute-start.24 = (f32[2,2,16,512]{3,2,1,0:T(8,128)S(1)}, f32[2,2,16,512]{3,2,1,0:T(8,128)S(1)}, u32[]{:S(2)}, u32[]{:S(2)}) collective-permute-start(f32[2,2,16,512]{3,2,1,0:T(8,128)S(1)} %get-tuple-element.32), channel_id=1, source_target_pairs={{0,32},{32,64},{64,96},{96,128},{128,160},{160,192},{192,224},{224... | collective-permute-start | bytes 393224 | tf_op jit(solution)/shard_map/ppermute | solution.py:20
  157.5 6.9 %collective-permute-start.25 = (f32[2,2,16,512]{3,2,1,0:T(8,128)S(1)}, f32[2,2,16,512]{3,2,1,0:T(8,128)S(1)}, u32[]{:S(2)}, u32[]{:S(2)}) collective-permute-start(f32[2,2,16,512]{3,2,1,0:T(8,128)S(1)} %get-tuple-element.33), channel_id=1, source_target_pairs={{32,0},{64,32},{96,64},{128,96},{160,128},{192,160},{224,192},{256... | collective-permute-start | bytes 393224 | tf_op jit(solution)/shard_map/ppermute | solution.py:23
  168.6 6.5 %collective-permute-start.27 = (f32[2,12,2,512]{3,2,1,0:T(2,128)S(1)}, f32[2,12,2,512]{3,2,1,0:T(2,128)S(1)}, u32[]{:S(2)}, u32[]{:S(2)}) collective-permute-start(f32[2,12,2,512]{3,2,1,0:T(2,128)S(1)} %get-tuple-element.19), channel_id=1, source_target_pairs={{4,0},{8,4},{12,8},{16,12},{20,16},{24,20},{28,24},{5,1},{9,5},{13... | collective-permute-start | bytes 294920 | tf_op jit(solution)/shard_map/ppermute | solution.py:23
  (15 other events, 117.9 us)
Sparse Core Ops, SparseCore 0:
  120.7 33.1 all-gather.2
  178.1 29.4 all-gather.4
where the time goes:
time: 500 us; the launch traced here: 499 us
  blocking collectives  306 us (61%)
  starting transfers between devices  76.5 us (15%)
  waiting for transfers between devices  75.5 us (15%)
  other arithmetic  22.2 us (4%)
  between operations  15.3 us (3%)
    psum x1, blocking collectives, local(): summed = lax.psum(pair_sums(velocity, everyone), ('gx', 'gz'))  306 us
    ppermute x14, waiting for transfers between devices, padded_2(): lax.ppermute(lax.slice_in_dim(block, 0, width, axis=dim), axis, backward)  60.9 us
    ppermute x14, starting transfers between devices, padded_2(): lax.ppermute(lax.slice_in_dim(block, block.shape[dim] - width, None, axis...  58 us
    ppermute x14, starting transfers between devices, padded_2(): lax.ppermute(lax.slice_in_dim(block, 0, width, axis=dim), axis, backward)  18.5 us
    ppermute x14, waiting for transfers between devices, padded_2(): lax.ppermute(lax.slice_in_dim(block, block.shape[dim] - width, None, axis...  14.6 us
  transfers between devices with their start and end apart: 30, of which 28 were waited for; matrix products, arithmetic and copies ran while one was open for 2% of the time, Pallas kernels for 0%

commit v1 on v0

v1 whole, which is shorter than its diff:
```python
import functools

import jax
import jax.numpy as jnp
from jax import lax
from jax.experimental import pallas as pl
from jax.experimental.pallas import tpu as pltpu
from jax.sharding import PartitionSpec as P


STEPS = 4
courant = 0.045
centre_coef = -7.5
near_coef = 4.0 / 3.0
far_coef = -1.0 / 12.0
middle = 1.5
ZC = 8
MESH = pl.DeviceIdType.MESH


def kernel(
    GX, GZ, PA, cells, NX, NZ,
    spread, vel_hbm, now_hbm, prev_hbm, obs_hbm, rec_hbm, out_hbm,
    natural, natural_obs, natural_rec, natural_out,
    U, V, C, W0, L, LAM, S, OB, MK,
    RV, AR, CUR, H, HR,
    in_sem, out_sem, halo_send, halo_recv, vel_send, vel_recv, ar_send, ar_recv,
    h_send, h_recv,
):
    gx, gz, pa = lax.axis_index("gx"), lax.axis_index("gz"), lax.axis_index("pa")
    core, hi = lax.rem(pa, 2), pa // 2
    partner = hi * 2 + (1 - core)
    across = (1 - hi) * 2 + core
    diagonal = (1 - hi) * 2 + (1 - core)

    loads = [
        pltpu.make_async_copy(now_hbm, natural.at[0], in_sem.at[0]),
        pltpu.make_async_copy(vel_hbm, natural.at[1], in_sem.at[1]),
        pltpu.make_async_copy(prev_hbm, natural.at[2], in_sem.at[2]),
        pltpu.make_async_copy(obs_hbm, natural_obs, in_sem.at[3]),
        pltpu.make_async_copy(rec_hbm, natural_rec, in_sem.at[4]),
    ]
    for load in loads:
        load.start()

    def turn(index, group, stride, step):
        low = lax.rem(index, stride)
        digit = lax.rem(index // stride, group)
        high = index // (stride * group)
        return (high * group + lax.rem(digit + step, group)) * stride + low

    stages = [
        [{"gx": turn(gx, 4, 1, j)} for j in (1, 2, 3)],
        [{"gx": turn(gx, GX // 4, 4, j)} for j in range(1, GX // 4)],
        [{"gz": turn(gz, 4, 1, j)} for j in (1, 2, 3)],
        [{"gz": turn(gz, GZ // 4, 4, j)} for j in range(1, GZ // 4)],
        [{"pa": turn(pa, 4, 1, j)} for j in (1, 2, 3)],
    ]
    halo_dest = [
        {"gx": lax.rem(gx + GX - 1, GX)},
        {"gx": lax.rem(gx + 1, GX)},
        {"gz": lax.rem(gz + GZ - 1, GZ)},
        {"gz": lax.rem(gz + 1, GZ)},
    ]
    sends_halo = [gx > 0, gx < GX - 1, gz > 0, gz < GZ - 1]
    gets_halo = [gx < GX - 1, gx > 0, gz < GZ - 1, gz > 0]

    barrier = pltpu.get_barrier_semaphore()
    for d in range(4):
        @pl.when(sends_halo[d])
        def _(d=d):
            pl.semaphore_signal(barrier, inc=1, device_id=halo_dest[d], device_id_type=MESH)
    count = 0
    for stage in stages:
        for peer in stage:
            pl.semaphore_signal(barrier, inc=1, device_id=peer, device_id_type=MESH)
            count += 1

    zero_x = jnp.zeros((2, NZ, 8, 128), jnp.float32)
    zero_z = jnp.zeros((NX, 2, 8, 128), jnp.float32)

    @pl.when(gx == 0)
    def _():
        for n in range(7):
            U[n, 0:2, 2 : NZ + 2] = zero_x

    @pl.when(gx == GX - 1)
    def _():
        for n in range(7):
            U[n, NX + 2 : NX + 4, 2 : NZ + 2] = zero_x

    @pl.when(gz == 0)
    def _():
        for n in range(7):
            U[n, 2 : NX + 2, 0:2] = zero_z

    @pl.when(gz == GZ - 1)
    def _():
        for n in range(7):
            U[n, 2 : NX + 2, NZ + 2 : NZ + 4] = zero_z

    def to_tiles(read, write):
        def plane(x, carry):
            for zt in range(NZ // 8):
                parts = [read(k, x, zt) for k in range(8)]
                write(x, zt * 8, jnp.swapaxes(jnp.stack(parts, axis=0), 0, 1))
            return carry
        lax.fori_loop(0, NX, plane, 0)

    def read_wave(slot):
        def read(k, x, zt):
            y = (k % 4) * 128
            return natural[slot, k // 4, x, zt * 8 : zt * 8 + 8, y : y + 128]
        return read

    def read_plain(ref):
        def read(k, x, zt):
            y = (k % 4) * 128
            return ref[x, zt * 8 : zt * 8 + 8, y : y + 128].astype(jnp.float32)
        return read

    def write_now(x, z, tiles):
        U[0, x + 2, z + 2 : z + 10] = tiles

    def write_velocity(x, z, tiles):
        V[x, z : z + 8] = tiles
        C[x, z : z + 8] = courant * tiles * tiles

    def write_prev(x, z, tiles):
        W0[x, z : z + 8] = tiles

    def write_obs(x, z, tiles):
        OB[x, z : z + 8] = tiles

    def write_mask(x, z, tiles):
        MK[x, z : z + 8] = tiles

    def halo(n, d):
        field = U.at[n]
        inner_x, inner_z = pl.ds(2, NX), pl.ds(2, NZ)
        source, target = [
            ((pl.ds(2, 2), inner_z), (pl.ds(NX + 2, 2), inner_z)),
            ((pl.ds(NX, 2), inner_z), (pl.ds(0, 2), inner_z)),
            ((inner_x, pl.ds(2, 2)), (inner_x, pl.ds(NZ + 2, 2))),
            ((inner_x, pl.ds(NZ, 2)), (inner_x, pl.ds(0, 2))),
        ][d]
        return pltpu.make_async_remote_copy(
            src_ref=field.at[source],
            dst_ref=field.at[target],
            send_sem=halo_send.at[n, d],
            recv_sem=halo_recv.at[n, d],
            device_id=halo_dest[d],
            device_id_type=MESH,
        )

    def send_halo(n, d):
        @pl.when(sends_halo[d])
        def _():
            halo(n, d).start()

    def wait_halo(n, d):
        @pl.when(gets_halo[d])
        def _():
            halo(n, d).wait_recv()

    loads[0].wait()
    to_tiles(read_wave(0), write_now)
    peers = count
    for gets in gets_halo:
        peers = peers + jnp.where(gets, 1, 0)
    pl.semaphore_wait(barrier, peers)
    for d in range(4):
        send_halo(0, d)

    loads[1].wait()
    to_tiles(read_wave(1), write_velocity)

    slab = NX // PA
    vel_copies = []
    for j in (1, 2, 3):
        q = lax.rem(pa + j, PA)
        vel_copies.append(
            pltpu.make_async_remote_copy(
                src_ref=V.at[pl.ds(q * slab, slab)],
                dst_ref=RV.at[j],
                send_sem=vel_send.at[j],
                recv_sem=vel_recv.at[j],
                device_id={"pa": q},
                device_id_type=MESH,
            )
        )
    for copy in vel_copies:
        copy.start()

    loads[2].wait()
    to_tiles(read_wave(2), write_prev)
    loads[3].wait()
    to_tiles(read_plain(natural_obs), write_obs)
    loads[4].wait()
    to_tiles(read_plain(natural_rec), write_mask)

    shape = (ZC, 8, 128)
    lane = lax.broadcasted_iota(jnp.int32, shape, 2)
    sub = lax.broadcasted_iota(jnp.int32, shape, 1)
    lane2 = lax.broadcasted_iota(jnp.int32, (8, 128), 1)
    sub2 = lax.broadcasted_iota(jnp.int32, (8, 128), 0)

    scale = (
        jnp.full((8, 128), spread[0], jnp.int32).astype(jnp.float32)
        / jnp.full((8, 128), spread[1], jnp.int32).astype(jnp.float32)
    )
    pull = 2.0 / scale

    def laplace(n, x, z):
        here = U[n, x + 2, pl.ds(z + 2, ZC)]
        near = U[n, x + 1, pl.ds(z + 2, ZC)] + U[n, x + 3, pl.ds(z + 2, ZC)]
        far = U[n, x, pl.ds(z + 2, ZC)] + U[n, x + 4, pl.ds(z + 2, ZC)]
        near = near + (U[n, x + 2, pl.ds(z + 1, ZC)] + U[n, x + 2, pl.ds(z + 3, ZC)])
        far = far + (U[n, x + 2, pl.ds(z, ZC)] + U[n, x + 2, pl.ds(z + 4, ZC)])
        before = pltpu.roll(here, 1, 1)
        before = jnp.where((sub == 0) | (sub == 4), 0.0, before)
        after = pltpu.roll(here, 7, 1)
        after = jnp.where((sub == 3) | (sub == 7), 0.0, after)
        near = near + (
            pltpu.roll(jnp.where(lane == 127, before, here), 1, 2)
            + pltpu.roll(jnp.where(lane == 0, after, here), 127, 2)
        )
        far = far + (
            pltpu.roll(jnp.where(lane >= 126, before, here), 2, 2)
            + pltpu.roll(jnp.where(lane <= 1, after, here), 126, 2)
        )
        return here, centre_coef * here + near_coef * near + far_coef * far

    def advance(n, x, z):
        here, applied = laplace(n, x, z)
        at = (x, pl.ds(z, ZC))
        inner = (x + 2, pl.ds(z + 2, ZC))
        if n < STEPS:
            older = W0[at] if n == 0 else U[(n - 1,) + inner]
            newer = 2.0 * here - older + C[at] * applied
            if n < STEPS - 1:
                L[(n,) + at] = applied
                U[(n + 1,) + inner] = newer
            else:
                adjoint = MK[at] * (newer - OB[at])
                S[at] = adjoint * applied
                LAM[(0,) + at] = adjoint
                U[(n + 1,) + inner] = C[at] * adjoint
        else:
            k = n - STEPS
            adjoint = 2.0 * LAM[(k,) + at] + applied
            if k > 0:
                adjoint = adjoint - LAM[(k - 1,) + at]
            total = S[at] + adjoint * L[(STEPS - 2 - k,) + at]
            if k < STEPS - 2:
                S[at] = total
                LAM[(k + 1,) + at] = adjoint
                U[(n + 1,) + inner] = C[at] * adjoint
            else:
                velocity = V[at]
                H[at] = (2.0 * courant) * velocity * total + pull[None] * (velocity - middle)

    def planes(n, first, count_x):
        per = NZ // ZC

        def body(i, carry):
            advance(n, first + i // per, lax.rem(i, per) * ZC)
            return carry
        lax.fori_loop(0, count_x * per, body, 0)

    def ar_copies(stage):
        return [
            pltpu.make_async_remote_copy(
                src_ref=CUR.at[stage],
                dst_ref=AR.at[stage, j],
                send_sem=ar_send.at[stage, j],
                recv_sem=ar_recv.at[stage, j],
                device_id=peer,
                device_id_type=MESH,
            )
            for j, peer in enumerate(stages[stage])
        ]

    def ar_start(stage):
        for copy in ar_copies(stage):
            copy.start()

    def ar_finish(stage):
        total = CUR[stage]
        for j, copy in enumerate(ar_copies(stage)):
            copy.wait_recv()
            total = total + AR[stage, j]
        CUR[stage + 1] = total

    def pair_sums():
        for copy in vel_copies:
            copy.wait_recv()

        def body(i, sums):
            x, z = i // NZ, lax.rem(i, NZ)
            tile = [V[pa * slab + x, z]] + [RV[j, x, z] for j in (1, 2, 3)]
            swapped = [pltpu.roll(t, 4, 0) for t in tile]
            out, at = [], 0
            for a in range(4):
                for b in range(a, 4):
                    if b > a:
                        delta = tile[a] - tile[b]
                        out.append(sums[at] + delta * delta)
                        at += 1
                    delta = tile[a] - swapped[b]
                    out.append(sums[at] + delta * delta)
                    at += 1
            return tuple(out)

        zero = jnp.zeros((8, 128), jnp.float32)
        sums = lax.fori_loop(0, slab * NZ, body, (zero,) * 16)
        groups = [lax.rem(pa + PA - j, PA) for j in range(4)]
        table, at = zero, 0
        for a in range(4):
            for b in range(a, 4):
                if b > a:
                    plain = jnp.sum(sums[at], axis=1, keepdims=True)
                    at += 1
                    spot = (lane2 == groups[a] * 8 + groups[b] * 2) | (lane2 == groups[b] * 8 + groups[a] * 2)
                    table = jnp.where(spot, plain, table)
                crossed = jnp.sum(sums[at], axis=1, keepdims=True)
                at += 1
                table = jnp.where(lane2 == groups[a] * 8 + groups[b] * 2 + 1, crossed, table)
                if b > a:
                    turned = pltpu.roll(jnp.broadcast_to(crossed, (8, 128)), 4, 0)
                    table = jnp.where(lane2 == groups[b] * 8 + groups[a] * 2 + 1, turned, table)
        CUR[0] = table

    def h_copy(kind, x, src, dest):
        return pltpu.make_async_remote_copy(
            src_ref=src,
            dst_ref=HR.at[kind, x],
            send_sem=h_send.at[kind, x],
            recv_sem=h_recv.at[kind, x],
            device_id={"pa": dest},
            device_id_type=MESH,
        )

    def h_own(x):
        return h_copy(0, x, H.at[x], partner)

    def h_across(x):
        return h_copy(1, x, H.at[x], across)

    def h_forward(x):
        return h_copy(2, x, HR.at[1, x], partner)

    for n in range(7):
        wait_halo(n, 2)
        wait_halo(n, 3)
        planes(n, 2, NX - 4)
        if n == 6:
            for x in range(2, NX - 2):
                h_across(x).start()
                h_own(x).start()
        wait_halo(n, 0)
        wait_halo(n, 1)
        planes(n, 0, 2)
        if n < 6:
            send_halo(n + 1, 0)
        else:
            for x in (0, 1):
                h_across(x).start()
                h_own(x).start()
        planes(n, NX - 2, 2)
        if n < 6:
            send_halo(n + 1, 1)
            send_halo(n + 1, 2)
            send_halo(n + 1, 3)
        else:
            for x in (NX - 2, NX - 1):
                h_across(x).start()
                h_own(x).start()
        if n == 1:
            pair_sums()
            ar_start(0)
        elif 2 <= n <= 5:
            ar_finish(n - 2)
            ar_start(n - 1)
    ar_finish(4)

    table = CUR[5]
    low = jnp.sum(jnp.where(sub2 < 4, table, 0.0), axis=0, keepdims=True)
    high = jnp.sum(jnp.where(sub2 < 4, 0.0, table), axis=0, keepdims=True)
    weight = jnp.exp(-(jnp.where(sub2 < 4, low, high) / cells) / scale)

    def column(index):
        picked = jnp.sum(jnp.where(lane2 == index, weight, 0.0), axis=1, keepdims=True)
        return jnp.broadcast_to(picked, (8, 128))

    groups = [pa, partner, across, diagonal]
    plain = [column(pa * 8 + g * 2) for g in groups]
    crossed = [column(pa * 8 + g * 2 + 1) for g in groups]
    all_weights = plain[0] + crossed[0]
    for g in (1, 2, 3):
        all_weights = all_weights + (plain[g] + crossed[g])
    count_all = 2 * PA
    own = pull * all_weights / count_all
    plain = [-w / count_all for w in plain]
    crossed = [-w / count_all for w in crossed]

    order = list(range(2, NX - 2)) + [0, 1, NX - 2, NX - 1]
    for x in order:
        h_across(x).wait_recv()
        h_forward(x).start()

    outs = []
    for at, x in enumerate(order):
        h_own(x).wait_recv()
        h_forward(x).wait_recv()
        for zt in range(NZ // 8):
            z = zt * 8
            result = own[None] * (V[x, z : z + 8] - middle)
            for g in range(4):
                tile = H[x, z : z + 8] if g == 0 else HR[g - 1, x, z : z + 8]
                result = result + plain[g][None] * tile + crossed[g][None] * pltpu.roll(tile, 4, 1)
            result = jnp.swapaxes(result, 0, 1)
            for k in range(8):
                y = (k % 4) * 128
                natural_out[k // 4, x, z : z + 8, y : y + 128] = result[k]
        copy = pltpu.make_async_copy(
            natural_out.at[:, pl.ds(x, 1)], out_hbm.at[:, pl.ds(x, 1)], out_sem.at[x]
        )
        copy.start()
        outs.append(copy)

    for n in range(7):
        for d in range(4):
            @pl.when(sends_halo[d])
            def _(n=n, d=d):
                halo(n, d).wait_send()
    for copy in vel_copies:
        copy.wait_send()
    for stage in range(5):
        for copy in ar_copies(stage):
            copy.wait_send()
    for x in order:
        h_across(x).wait_send()
        h_own(x).wait_send()
        h_forward(x).wait_send()
    for copy in outs:
        copy.wait()


def local(velocity, wave_now, wave_prev, observed, receiver, spread):
    GX, GZ, PA = lax.axis_size("gx"), lax.axis_size("gz"), lax.axis_size("pa")
    particles, NX, NZ, NY = velocity.shape
    cells = float(NX * GX * NZ * GZ * NY)
    any_space = pl.BlockSpec(memory_space=pl.ANY)
    tiles = (NX, NZ, 8, 128)
    f32 = jnp.float32
    dma = pltpu.SemaphoreType.DMA
    return pl.pallas_call(
        functools.partial(kernel, GX, GZ, PA, cells, NX, NZ),
        out_shape=jax.ShapeDtypeStruct(velocity.shape, f32),
        in_specs=[pl.BlockSpec(memory_space=pltpu.SMEM)] + [any_space] * 5,
        out_specs=any_space,
        scratch_shapes=[
            pltpu.VMEM((3,) + velocity.shape, f32),
            pltpu.VMEM(observed.shape, f32),
            pltpu.VMEM(receiver.shape, jnp.int32),
            pltpu.VMEM(velocity.shape, f32),
            pltpu.VMEM((7, NX + 4, NZ + 4, 8, 128), f32),
            pltpu.VMEM(tiles, f32),
            pltpu.VMEM(tiles, f32),
            pltpu.VMEM(tiles, f32),
            pltpu.VMEM((3,) + tiles, f32),
            pltpu.VMEM((3,) + tiles, f32),
            pltpu.VMEM(tiles, f32),
            pltpu.VMEM(tiles, f32),
            pltpu.VMEM(tiles, f32),
            pltpu.VMEM((4, NX // PA, NZ, 8, 128), f32),
            pltpu.VMEM((5, 3, 8, 128), f32),
            pltpu.VMEM((6, 8, 128), f32),
            pltpu.VMEM(tiles, f32),
            pltpu.VMEM((3,) + tiles, f32),
            dma((5,)),
            dma((NX,)),
            dma((7, 4)),
            dma((7, 4)),
            dma((4,)),
            dma((4,)),
            dma((5, 3)),
            dma((5, 3)),
            dma((3, NX)),
            dma((3, NX)),
        ],
        compiler_params=pltpu.CompilerParams(collective_id=0, has_side_effects=True),
    )(spread, velocity, wave_now, wave_prev, observed, receiver)


def solution(mesh):
    in_specs = (
        P("pa", "gx", "gz", None),
        P("pa", "gx", "gz", None),
        P("pa", "gx", "gz", None),
        P("gx", "gz", None),
        P("gx", "gz", None),
        P(),
    )
    out_specs = P("pa", "gx", "gz", None)
    return jax.shard_map(local, mesh=mesh, in_specs=in_specs, out_specs=out_specs, check_vma=False)
```

time: 500 us -> 74.2 us (0.15)
  the two profiles are of different devices: /device:TPU:16 before, /device:TPU:8 now
where the time goes in v1:
time: 74.2 us; the launch traced here: 73 us
  Pallas kernels  71.1 us (96%)
  local copies, waits for them, and re-layouts  1.88 us (3%)
    pallas_call x1, Pallas kernels, local(): pl.pallas_call(functools.partial(kernel, GX, GZ, PA, cells, NX, NZ), out_...  71.1 us
    unnamed x1, local copies, waits for them, and re-layouts  1.88 us

profile of v1, /device:TPU:8, one launch (start us, length us, event | category | flops | bytes accessed | tf_op | source)
XLA Modules:
  0.0 73.0 jit_solution(6835964350044649274)
XLA Ops:
  0.0 71.1 %shard_map.64 = f32[2,8,16,512]{3,2,1,0:T(8,128)} custom-call(s32[2]{0:T(128)} %spread.1, f32[2,8,16,512]{3,2,1,0:T(8,128)} %vel_hbm.1, f32[2,8,16,512]{3,2,1,0:T(8,128)} %now_hbm.1, f32[2,8,16,512]{3,2,1,0:T(8,128)} %prev_hbm.1, f32[8,16,512]{2,1,0:T(8,128)} %obs_hbm.1, s32[8,16,512]{2,1,0:T(8,128)} %rec_hbm.1), custom_call_target="tpu_custom_call" | custom-call | tf_op jit(solution)/shard_map/pallas_call | solution.py:458
  71.1 1.9 %copy.8 = f32[2,8,16,512]{3,2,1,0:T(8,128)} copy(f32[2,8,16,512]{3,2,1,0:T(8,128)} %shard_map.64) | data formatting | bytes 1048576

commit v2 on v1

--- a/solution.py
+++ b/solution.py
@@ -50,26 +50,28 @@
         return (high * group + lax.rem(digit + step, group)) * stride + low
 
     stages = [
+        [{"pa": turn(pa, 4, 1, j)} for j in (1, 2, 3)],
+        [{"gz": turn(gz, GZ // 4, 4, j)} for j in range(1, GZ // 4)],
+        [{"gz": turn(gz, 4, 1, j)} for j in (1, 2, 3)],
         [{"gx": turn(gx, 4, 1, j)} for j in (1, 2, 3)],
         [{"gx": turn(gx, GX // 4, 4, j)} for j in range(1, GX // 4)],
-        [{"gz": turn(gz, 4, 1, j)} for j in (1, 2, 3)],
-        [{"gz": turn(gz, GZ // 4, 4, j)} for j in range(1, GZ // 4)],
-        [{"pa": turn(pa, 4, 1, j)} for j in (1, 2, 3)],
     ]
-    halo_dest = [
-        {"gx": lax.rem(gx + GX - 1, GX)},
-        {"gx": lax.rem(gx + 1, GX)},
-        {"gz": lax.rem(gz + GZ - 1, GZ)},
-        {"gz": lax.rem(gz + 1, GZ)},
-    ]
-    sends_halo = [gx > 0, gx < GX - 1, gz > 0, gz < GZ - 1]
-    gets_halo = [gx < GX - 1, gx > 0, gz < GZ - 1, gz > 0]
+    half = [lax.rem(gz, 2), 1 - lax.rem(gz, 2)]
+    z_side = [gz + 2 * h - 1 for h in half]
+    has_low, has_high = gx > 0, gx < GX - 1
+    has_side = [(side >= 0) & (side < GZ) for side in z_side]
+    low_dest = {"gx": lax.rem(gx + GX - 1, GX)}
+    high_dest = {"gx": lax.rem(gx + 1, GX)}
+    side_dest = [{"gz": lax.rem(side + GZ, GZ)} for side in z_side]
+    sends_halo = [has_low, has_high] + has_side
+    gets_halo = [has_high, has_low] + has_side
+    greet = [low_dest, high_dest] + side_dest
 
     barrier = pltpu.get_barrier_semaphore()
     for d in range(4):
         @pl.when(sends_halo[d])
         def _(d=d):
-            pl.semaphore_signal(barrier, inc=1, device_id=halo_dest[d], device_id_type=MESH)
+            pl.semaphore_signal(barrier, inc=1, device_id=greet[d], device_id_type=MESH)
     count = 0
     for stage in stages:
         for peer in stage:
@@ -99,13 +101,13 @@
         for n in range(7):
             U[n, 2 : NX + 2, NZ + 2 : NZ + 4] = zero_z
 
-    def to_tiles(read, write):
+    def to_tiles(read, write, first=0, planes=NX):
         def plane(x, carry):
             for zt in range(NZ // 8):
                 parts = [read(k, x, zt) for k in range(8)]
                 write(x, zt * 8, jnp.swapaxes(jnp.stack(parts, axis=0), 0, 1))
             return carry
-        lax.fori_loop(0, NX, plane, 0)
+        lax.fori_loop(first, first + planes, plane, 0)
 
     def read_wave(slot):
         def read(k, x, zt):
@@ -135,42 +137,51 @@
     def write_mask(x, z, tiles):
         MK[x, z : z + 8] = tiles
 
-    def halo(n, d):
+    def halo(n, s, d):
         field = U.at[n]
-        inner_x, inner_z = pl.ds(2, NX), pl.ds(2, NZ)
-        source, target = [
-            ((pl.ds(2, 2), inner_z), (pl.ds(NX + 2, 2), inner_z)),
-            ((pl.ds(NX, 2), inner_z), (pl.ds(0, 2), inner_z)),
-            ((inner_x, pl.ds(2, 2)), (inner_x, pl.ds(NZ + 2, 2))),
-            ((inner_x, pl.ds(NZ, 2)), (inner_x, pl.ds(0, 2))),
+        rows = pl.ds(2 + half[s] * ZC, ZC)
+        inner = pl.ds(2, NX)
+        source, target, dest = [
+            ((pl.ds(2, 2), rows), (pl.ds(NX + 2, 2), rows), low_dest),
+            ((pl.ds(NX, 2), rows), (pl.ds(0, 2), rows), high_dest),
+            (
+                (inner, pl.ds(2 + half[s] * (NZ - 2), 2)),
+                (inner, pl.ds((1 - half[s]) * (NZ + 2), 2)),
+                side_dest[s],
+            ),
         ][d]
         return pltpu.make_async_remote_copy(
             src_ref=field.at[source],
             dst_ref=field.at[target],
-            send_sem=halo_send.at[n, d],
-            recv_sem=halo_recv.at[n, d],
-            device_id=halo_dest[d],
+            send_sem=halo_send.at[n, s * 3 + d],
+            recv_sem=halo_recv.at[n, s * 3 + d],
+            device_id=dest,
             device_id_type=MESH,
         )
 
-    def send_halo(n, d):
-        @pl.when(sends_halo[d])
+    def send_halo(n, s, d):
+        @pl.when(sends_halo[d if d < 2 else 2 + s])
         def _():
-            halo(n, d).start()
-
-    def wait_halo(n, d):
-        @pl.when(gets_halo[d])
+            halo(n, s, d).start()
+
+    def wait_halo(n, s, d):
+        @pl.when(gets_halo[d if d < 2 else 2 + s])
         def _():
-            halo(n, d).wait_recv()
+            halo(n, s, d).wait_recv()
 
     loads[0].wait()
-    to_tiles(read_wave(0), write_now)
+    to_tiles(read_wave(0), write_now, 0, 2)
+    to_tiles(read_wave(0), write_now, NX - 2, 2)
     peers = count
     for gets in gets_halo:
         peers = peers + jnp.where(gets, 1, 0)
     pl.semaphore_wait(barrier, peers)
-    for d in range(4):
-        send_halo(0, d)
+    for s in (0, 1):
+        for d in (0, 1):
+            send_halo(0, s, d)
+    to_tiles(read_wave(0), write_now, 2, NX - 4)
+    for s in (0, 1):
+        send_halo(0, s, 2)
 
     loads[1].wait()
     to_tiles(read_wave(1), write_velocity)
@@ -260,13 +271,11 @@
                 velocity = V[at]
                 H[at] = (2.0 * courant) * velocity * total + pull[None] * (velocity - middle)
 
-    def planes(n, first, count_x):
-        per = NZ // ZC
-
-        def body(i, carry):
-            advance(n, first + i // per, lax.rem(i, per) * ZC)
+    def planes(n, s, first, count_x):
+        def body(x, carry):
+            advance(n, x, half[s] * ZC)
             return carry
-        lax.fori_loop(0, count_x * per, body, 0)
+        lax.fori_loop(first, first + count_x, body, 0)
 
     def ar_copies(stage):
         return [
@@ -331,57 +340,65 @@
                     table = jnp.where(lane2 == groups[b] * 8 + groups[a] * 2 + 1, turned, table)
         CUR[0] = table
 
-    def h_copy(kind, x, src, dest):
+    firsts = [2, 4, 0, NX - 2]
+
+    def chunk(c):
+        return pl.ds(firsts[c % 4], 2), pl.ds(half[c // 4] * ZC, ZC)
+
+    def h_copy(kind, c, src, dest):
         return pltpu.make_async_remote_copy(
             src_ref=src,
-            dst_ref=HR.at[kind, x],
-            send_sem=h_send.at[kind, x],
-            recv_sem=h_recv.at[kind, x],
+            dst_ref=HR.at[kind, c],
+            send_sem=h_send.at[kind, c],
+            recv_sem=h_recv.at[kind, c],
             device_id={"pa": dest},
             device_id_type=MESH,
         )
 
-    def h_own(x):
-        return h_copy(0, x, H.at[x], partner)
-
-    def h_across(x):
-        return h_copy(1, x, H.at[x], across)
-
-    def h_forward(x):
-        return h_copy(2, x, HR.at[1, x], partner)
+    def h_own(c):
+        return h_copy(0, c, H.at[chunk(c)], partner)
+
+    def h_across(c):
+        return h_copy(1, c, H.at[chunk(c)], across)
+
+    def h_forward(c):
+        return h_copy(2, c, HR.at[1, c], partner)
+
+    def h_start(c):
+        h_across(c).start()
+        h_own(c).start()
 
     for n in range(7):
-        wait_halo(n, 2)
-        wait_halo(n, 3)
-        planes(n, 2, NX - 4)
-        if n == 6:
-            for x in range(2, NX - 2):
-                h_across(x).start()
-                h_own(x).start()
-        wait_halo(n, 0)
-        wait_halo(n, 1)
-        planes(n, 0, 2)
-        if n < 6:
-            send_halo(n + 1, 0)
-        else:
-            for x in (0, 1):
-                h_across(x).start()
-                h_own(x).start()
-        planes(n, NX - 2, 2)
-        if n < 6:
-            send_halo(n + 1, 1)
-            send_halo(n + 1, 2)
-            send_halo(n + 1, 3)
-        else:
-            for x in (NX - 2, NX - 1):
-                h_across(x).start()
-                h_own(x).start()
-        if n == 1:
+        for s in (0, 1):
+            wait_halo(n, s, 2)
+            planes(n, s, 2, NX - 4)
+            if n == 6:
+                h_start(4 * s)
+                h_start(4 * s + 1)
+            wait_halo(n, s, 0)
+            wait_halo(n, s, 1)
+            planes(n, s, 0, 2)
+            if n < 6:
+                send_halo(n + 1, s, 0)
+            else:
+                h_start(4 * s + 2)
+            planes(n, s, NX - 2, 2)
+            if n < 6:
+                send_halo(n + 1, s, 1)
+                send_halo(n + 1, s, 2)
+            else:
+                h_start(4 * s + 3)
+        if n == 2:
             pair_sums()
             ar_start(0)
-        elif 2 <= n <= 5:
-            ar_finish(n - 2)
-            ar_start(n - 1)
+        elif n > 2:
+            ar_finish(n - 3)
+            ar_start(n - 2)
+
+    chunks = range(8)
+    for c in chunks:
+        h_across(c).wait_recv()
+        h_forward(c).start()
     ar_finish(4)
 
     table = CUR[5]
@@ -404,45 +421,41 @@
     plain = [-w / count_all for w in plain]
     crossed = [-w / count_all for w in crossed]
 
-    order = list(range(2, NX - 2)) + [0, 1, NX - 2, NX - 1]
-    for x in order:
-        h_across(x).wait_recv()
-        h_forward(x).start()
-
     outs = []
-    for at, x in enumerate(order):
-        h_own(x).wait_recv()
-        h_forward(x).wait_recv()
-        for zt in range(NZ // 8):
-            z = zt * 8
-            result = own[None] * (V[x, z : z + 8] - middle)
+    for c in chunks:
+        h_own(c).wait_recv()
+        h_forward(c).wait_recv()
+        x0, z = firsts[c % 4], pl.multiple_of(half[c // 4] * ZC, ZC)
+        for i in range(2):
+            x = x0 + i
+            result = own[None] * (V[x, pl.ds(z, ZC)] - middle)
             for g in range(4):
-                tile = H[x, z : z + 8] if g == 0 else HR[g - 1, x, z : z + 8]
+                tile = H[x, pl.ds(z, ZC)] if g == 0 else HR[g - 1, c, i]
                 result = result + plain[g][None] * tile + crossed[g][None] * pltpu.roll(tile, 4, 1)
             result = jnp.swapaxes(result, 0, 1)
             for k in range(8):
                 y = (k % 4) * 128
-                natural_out[k // 4, x, z : z + 8, y : y + 128] = result[k]
-        copy = pltpu.make_async_copy(
-            natural_out.at[:, pl.ds(x, 1)], out_hbm.at[:, pl.ds(x, 1)], out_sem.at[x]
-        )
+                natural_out[k // 4, x, pl.ds(z, ZC), y : y + 128] = result[k]
+        at = (slice(None), pl.ds(x0, 2), pl.ds(z, ZC))
+        copy = pltpu.make_async_copy(natural_out.at[at], out_hbm.at[at], out_sem.at[c])
         copy.start()
         outs.append(copy)
 
     for n in range(7):
-        for d in range(4):
-            @pl.when(sends_halo[d])
-            def _(n=n, d=d):
-                halo(n, d).wait_send()
+        for s in (0, 1):
+            for d in range(3):
+                @pl.when(sends_halo[d if d < 2 else 2 + s])
+                def _(n=n, s=s, d=d):
+                    halo(n, s, d).wait_send()
     for copy in vel_copies:
         copy.wait_send()
     for stage in range(5):
         for copy in ar_copies(stage):
             copy.wait_send()
-    for x in order:
-        h_across(x).wait_send()
-        h_own(x).wait_send()
-        h_forward(x).wait_send()
+    for c in chunks:
+        h_across(c).wait_send()
+        h_own(c).wait_send()
+        h_forward(c).wait_send()
     for copy in outs:
         copy.wait()
 
@@ -478,17 +491,17 @@
             pltpu.VMEM((5, 3, 8, 128), f32),
             pltpu.VMEM((6, 8, 128), f32),
             pltpu.VMEM(tiles, f32),
-            pltpu.VMEM((3,) + tiles, f32),
+            pltpu.VMEM((3, 8, 2, ZC, 8, 128), f32),
             dma((5,)),
-            dma((NX,)),
-            dma((7, 4)),
-            dma((7, 4)),
+            dma((8,)),
+            dma((7, 6)),
+            dma((7, 6)),
             dma((4,)),
             dma((4,)),
             dma((5, 3)),
             dma((5, 3)),
-            dma((3, NX)),
-            dma((3, NX)),
+            dma((3, 8)),
+            dma((3, 8)),
         ],
         compiler_params=pltpu.CompilerParams(collective_id=0, has_side_effects=True),
     )(spread, velocity, wave_now, wave_prev, observed, receiver)

time: 74.2 us -> 68.7 us (0.926)
  Pallas kernels: 71.1 us -> 65.7 us
    pallas_call x1, Pallas kernels: 71.1 us -> 65.7 us  [local(): pl.pallas_call(functools.partial(kernel, GX, GZ, PA, cells, NX, NZ), out_...]
where the time goes in v2:
time: 68.7 us; the launch traced here: 67.6 us
  Pallas kernels  65.7 us (96%)
  local copies, waits for them, and re-layouts  1.88 us (3%)
    pallas_call x1, Pallas kernels, local(): pl.pallas_call(functools.partial(kernel, GX, GZ, PA, cells, NX, NZ), out_...  65.7 us
    unnamed x1, local copies, waits for them, and re-layouts  1.88 us

profile of v2, /device:TPU:8, one launch (start us, length us, event | category | flops | bytes accessed | tf_op | source)
XLA Modules:
  0.0 67.6 jit_solution(8745788356132101340)
XLA Ops:
  0.0 65.7 %shard_map.64 = f32[2,8,16,512]{3,2,1,0:T(8,128)} custom-call(s32[2]{0:T(128)} %spread.1, f32[2,8,16,512]{3,2,1,0:T(8,128)} %vel_hbm.1, f32[2,8,16,512]{3,2,1,0:T(8,128)} %now_hbm.1, f32[2,8,16,512]{3,2,1,0:T(8,128)} %prev_hbm.1, f32[8,16,512]{2,1,0:T(8,128)} %obs_hbm.1, s32[8,16,512]{2,1,0:T(8,128)} %rec_hbm.1), custom_call_target="tpu_custom_call" | custom-call | tf_op jit(solution)/shard_map/pallas_call | solution.py:471
  65.7 1.9 %copy.8 = f32[2,8,16,512]{3,2,1,0:T(8,128)} copy(f32[2,8,16,512]{3,2,1,0:T(8,128)} %shard_map.64) | data formatting | bytes 1048576

commit v3 on v2

--- a/solution.py
+++ b/solution.py
@@ -23,9 +23,9 @@
     spread, vel_hbm, now_hbm, prev_hbm, obs_hbm, rec_hbm, out_hbm,
     natural, natural_obs, natural_rec, natural_out,
     U, V, C, W0, L, LAM, S, OB, MK,
-    RV, AR, CUR, H, HR,
+    RV, AR, CUR, H, HR, RL,
     in_sem, out_sem, halo_send, halo_recv, vel_send, vel_recv, ar_send, ar_recv,
-    h_send, h_recv,
+    h_send, h_recv, relay_send, relay_recv,
 ):
     gx, gz, pa = lax.axis_index("gx"), lax.axis_index("gz"), lax.axis_index("pa")
     core, hi = lax.rem(pa, 2), pa // 2
@@ -77,6 +77,11 @@
         for peer in stage:
             pl.semaphore_signal(barrier, inc=1, device_id=peer, device_id_type=MESH)
             count += 1
+    beside = lax.rem(gz + 4, GZ)
+    pl.semaphore_signal(
+        barrier, inc=1, device_id={"gz": beside, "pa": across}, device_id_type=MESH
+    )
+    count += 1
 
     zero_x = jnp.zeros((2, NZ, 8, 128), jnp.float32)
     zero_z = jnp.zeros((NX, 2, 8, 128), jnp.float32)
@@ -358,6 +363,37 @@
     def h_own(c):
         return h_copy(0, c, H.at[chunk(c)], partner)
 
+    def h_relay(c):
+        return pltpu.make_async_remote_copy(
+            src_ref=H.at[chunk(c)],
+            dst_ref=RL.at[hi, c // 2],
+            send_sem=relay_send.at[c],
+            recv_sem=relay_recv.at[hi, c // 2],
+            device_id={"gz": beside, "pa": (c % 2) * 2 + core},
+            device_id_type=MESH,
+        )
+
+    def relayed(source, i):
+        return pltpu.make_async_remote_copy(
+            src_ref=H.at[chunk(2 * i)],
+            dst_ref=RL.at[source, i],
+            send_sem=relay_send.at[2 * i],
+            recv_sem=relay_recv.at[source, i],
+            device_id={"gz": beside, "pa": source * 2 + core},
+            device_id_type=MESH,
+        )
+
+    def h_pass(source, i):
+        c = 2 * i + hi
+        return pltpu.make_async_remote_copy(
+            src_ref=RL.at[source, i],
+            dst_ref=HR.at[1, c],
+            send_sem=relay_send.at[8 + source * 4 + i],
+            recv_sem=h_recv.at[1, c],
+            device_id={"gz": beside, "pa": (1 - source) * 2 + core},
+            device_id_type=MESH,
+        )
+
     def h_across(c):
         return h_copy(1, c, H.at[chunk(c)], across)
 
@@ -365,7 +401,7 @@
         return h_copy(2, c, HR.at[1, c], partner)
 
     def h_start(c):
-        h_across(c).start()
+        h_relay(c).start()
         h_own(c).start()
 
     for n in range(7):
@@ -396,9 +432,24 @@
             ar_start(n - 2)
 
     chunks = range(8)
-    for c in chunks:
-        h_across(c).wait_recv()
-        h_forward(c).start()
+    def pass_on(i):
+        for source in (0, 1):
+            relayed(source, i).wait_recv()
+            h_pass(source, i).start()
+
+    def forward(i):
+        for c in (2 * i, 2 * i + 1):
+            h_across(c).wait_recv()
+            h_forward(c).start()
+
+    pass_on(0)
+    pass_on(1)
+    forward(0)
+    pass_on(2)
+    forward(1)
+    pass_on(3)
+    forward(2)
+    forward(3)
     ar_finish(4)
 
     table = CUR[5]
@@ -453,7 +504,8 @@
         for copy in ar_copies(stage):
             copy.wait_send()
     for c in chunks:
-        h_across(c).wait_send()
+        h_relay(c).wait_send()
+        h_pass(c // 4, c % 4).wait_send()
         h_own(c).wait_send()
         h_forward(c).wait_send()
     for copy in outs:
@@ -492,6 +544,7 @@
             pltpu.VMEM((6, 8, 128), f32),
             pltpu.VMEM(tiles, f32),
             pltpu.VMEM((3, 8, 2, ZC, 8, 128), f32),
+            pltpu.VMEM((2, 4, 2, ZC, 8, 128), f32),
             dma((5,)),
             dma((8,)),
             dma((7, 6)),
@@ -502,6 +555,8 @@
             dma((5, 3)),
             dma((3, 8)),
             dma((3, 8)),
+            dma((16,)),
+            dma((2, 4)),
         ],
         compiler_params=pltpu.CompilerParams(collective_id=0, has_side_effects=True),
     )(spread, velocity, wave_now, wave_prev, observed, receiver)

time: 68.7 us -> 74 us (1.077)
  the two profiles are of different devices: /device:TPU:8 before, /device:TPU:1 now
where the time goes in v3:
time: 74 us; the launch traced here: 73.8 us
  Pallas kernels  71.9 us (97%)
  local copies, waits for them, and re-layouts  1.88 us (3%)
    pallas_call x1, Pallas kernels, local(): pl.pallas_call(functools.partial(kernel, GX, GZ, PA, cells, NX, NZ), out_...  71.9 us
    unnamed x1, local copies, waits for them, and re-layouts  1.88 us

profile of v3, /device:TPU:1, one launch (start us, length us, event | category | flops | bytes accessed | tf_op | source)
XLA Modules:
  0.0 73.8 jit_solution(15118845503479812826)
XLA Ops:
  0.0 71.9 %shard_map.64 = f32[2,8,16,512]{3,2,1,0:T(8,128)} custom-call(s32[2]{0:T(128)} %spread.1, f32[2,8,16,512]{3,2,1,0:T(8,128)} %vel_hbm.1, f32[2,8,16,512]{3,2,1,0:T(8,128)} %now_hbm.1, f32[2,8,16,512]{3,2,1,0:T(8,128)} %prev_hbm.1, f32[8,16,512]{2,1,0:T(8,128)} %obs_hbm.1, s32[8,16,512]{2,1,0:T(8,128)} %rec_hbm.1), custom_call_target="tpu_custom_call" | custom-call | tf_op jit(solution)/shard_map/pallas_call | solution.py:523
  71.9 1.9 %copy.8 = f32[2,8,16,512]{3,2,1,0:T(8,128)} copy(f32[2,8,16,512]{3,2,1,0:T(8,128)} %shard_map.64) | data formatting | bytes 1048576

commit v4 on v2

--- a/solution.py
+++ b/solution.py
@@ -49,12 +49,15 @@
         high = index // (stride * group)
         return (high * group + lax.rem(digit + step, group)) * stride + low
 
+    def flip(index, stride):
+        return index + stride * (1 - 2 * lax.rem(index // stride, 2))
+
     stages = [
-        [{"pa": turn(pa, 4, 1, j)} for j in (1, 2, 3)],
-        [{"gz": turn(gz, GZ // 4, 4, j)} for j in range(1, GZ // 4)],
-        [{"gz": turn(gz, 4, 1, j)} for j in (1, 2, 3)],
+        [{"pa": turn(pa, PA, 1, j)} for j in range(1, PA)],
+        [{"gz": turn(gz, GZ, 1, j)} for j in range(1, GZ)],
         [{"gx": turn(gx, 4, 1, j)} for j in (1, 2, 3)],
-        [{"gx": turn(gx, GX // 4, 4, j)} for j in range(1, GX // 4)],
+        [{"gx": flip(gx, 4)}],
+        [{"gx": flip(gx, 8)}],
     ]
     half = [lax.rem(gz, 2), 1 - lax.rem(gz, 2)]
     z_side = [gz + 2 * h - 1 for h in half]
@@ -73,7 +76,7 @@
         def _(d=d):
             pl.semaphore_signal(barrier, inc=1, device_id=greet[d], device_id_type=MESH)
     count = 0
-    for stage in stages:
+    for stage in stages[:2]:
         for peer in stage:
             pl.semaphore_signal(barrier, inc=1, device_id=peer, device_id_type=MESH)
             count += 1
@@ -488,7 +491,7 @@
             pltpu.VMEM(tiles, f32),
             pltpu.VMEM(tiles, f32),
             pltpu.VMEM((4, NX // PA, NZ, 8, 128), f32),
-            pltpu.VMEM((5, 3, 8, 128), f32),
+            pltpu.VMEM((5, GZ - 1, 8, 128), f32),
             pltpu.VMEM((6, 8, 128), f32),
             pltpu.VMEM(tiles, f32),
             pltpu.VMEM((3, 8, 2, ZC, 8, 128), f32),
@@ -498,8 +501,8 @@
             dma((7, 6)),
             dma((4,)),
             dma((4,)),
-            dma((5, 3)),
-            dma((5, 3)),
+            dma((5, GZ - 1)),
+            dma((5, GZ - 1)),
             dma((3, 8)),
             dma((3, 8)),
         ],

time: 68.7 us -> 65.1 us (0.948); the launches traced: 67.6 us -> 64.9 us
  Pallas kernels: 65.7 us -> 63 us
    pallas_call x1, Pallas kernels: 65.7 us -> 63 us  [local(): pl.pallas_call(functools.partial(kernel, GX, GZ, PA, cells, NX, NZ), out_...]
where the time goes in v4:
time: 65.1 us; the launch traced here: 64.9 us
  Pallas kernels  63 us (97%)
  local copies, waits for them, and re-layouts  1.88 us (3%)
    pallas_call x1, Pallas kernels, local(): pl.pallas_call(functools.partial(kernel, GX, GZ, PA, cells, NX, NZ), out_...  63 us
    unnamed x1, local copies, waits for them, and re-layouts  1.88 us

profile of v4, /device:TPU:8, one launch (start us, length us, event | category | flops | bytes accessed | tf_op | source)
XLA Modules:
  0.0 64.9 jit_solution(1229496836275607354)
XLA Ops:
  0.0 63.0 %shard_map.64 = f32[2,8,16,512]{3,2,1,0:T(8,128)} custom-call(s32[2]{0:T(128)} %spread.1, f32[2,8,16,512]{3,2,1,0:T(8,128)} %vel_hbm.1, f32[2,8,16,512]{3,2,1,0:T(8,128)} %now_hbm.1, f32[2,8,16,512]{3,2,1,0:T(8,128)} %prev_hbm.1, f32[8,16,512]{2,1,0:T(8,128)} %obs_hbm.1, s32[8,16,512]{2,1,0:T(8,128)} %rec_hbm.1), custom_call_target="tpu_custom_call" | custom-call | tf_op jit(solution)/shard_map/pallas_call | solution.py:474
  63.1 1.9 %copy.8 = f32[2,8,16,512]{3,2,1,0:T(8,128)} copy(f32[2,8,16,512]{3,2,1,0:T(8,128)} %shard_map.64) | data formatting | bytes 1048576

commit v5 on v4

--- a/solution.py
+++ b/solution.py
@@ -278,7 +278,7 @@
         def body(x, carry):
             advance(n, x, half[s] * ZC)
             return carry
-        lax.fori_loop(first, first + count_x, body, 0)
+        lax.fori_loop(first, first + count_x, body, 0, unroll=count_x == 2)
 
     def ar_copies(stage):
         return [
@@ -391,12 +391,12 @@
                 send_halo(n + 1, s, 2)
             else:
                 h_start(4 * s + 3)
-        if n == 2:
-            pair_sums()
-            ar_start(0)
-        elif n > 2:
-            ar_finish(n - 3)
-            ar_start(n - 2)
+            if s == 0 and n == 2:
+                pair_sums()
+                ar_start(0)
+            elif s == 0 and n > 2:
+                ar_finish(n - 3)
+                ar_start(n - 2)
 
     chunks = range(8)
     for c in chunks:

time: 65.1 us -> 63 us (0.968)
  Pallas kernels: 63 us -> 60.9 us
    pallas_call x1, Pallas kernels: 63 us -> 60.9 us  [local(): pl.pallas_call(functools.partial(kernel, GX, GZ, PA, cells, NX, NZ), out_...]
where the time goes in v5:
time: 63 us; the launch traced here: 62.8 us
  Pallas kernels  60.9 us (97%)
  local copies, waits for them, and re-layouts  1.88 us (3%)
    pallas_call x1, Pallas kernels, local(): pl.pallas_call(functools.partial(kernel, GX, GZ, PA, cells, NX, NZ), out_...  60.9 us
    unnamed x1, local copies, waits for them, and re-layouts  1.88 us

profile of v5, /device:TPU:8, one launch (start us, length us, event | category | flops | bytes accessed | tf_op | source)
XLA Modules:
  0.0 62.8 jit_solution(5354793395672406286)
XLA Ops:
  0.0 60.9 %shard_map.64 = f32[2,8,16,512]{3,2,1,0:T(8,128)} custom-call(s32[2]{0:T(128)} %spread.1, f32[2,8,16,512]{3,2,1,0:T(8,128)} %vel_hbm.1, f32[2,8,16,512]{3,2,1,0:T(8,128)} %now_hbm.1, f32[2,8,16,512]{3,2,1,0:T(8,128)} %prev_hbm.1, f32[8,16,512]{2,1,0:T(8,128)} %obs_hbm.1, s32[8,16,512]{2,1,0:T(8,128)} %rec_hbm.1), custom_call_target="tpu_custom_call" | custom-call | tf_op jit(solution)/shard_map/pallas_call | solution.py:474
  60.9 1.9 %copy.8 = f32[2,8,16,512]{3,2,1,0:T(8,128)} copy(f32[2,8,16,512]{3,2,1,0:T(8,128)} %shard_map.64) | data formatting | bytes 1048576

commit v6 on v5

--- a/solution.py
+++ b/solution.py
@@ -399,9 +399,13 @@
                 ar_start(n - 2)
 
     chunks = range(8)
-    for c in chunks:
+
+    def forward(c):
         h_across(c).wait_recv()
         h_forward(c).start()
+
+    for c in range(6):
+        forward(c)
     ar_finish(4)
 
     table = CUR[5]
@@ -425,7 +429,8 @@
     crossed = [-w / count_all for w in crossed]
 
     outs = []
-    for c in chunks:
+
+    def combine(c):
         h_own(c).wait_recv()
         h_forward(c).wait_recv()
         x0, z = firsts[c % 4], pl.multiple_of(half[c // 4] * ZC, ZC)
@@ -443,6 +448,14 @@
         copy = pltpu.make_async_copy(natural_out.at[at], out_hbm.at[at], out_sem.at[c])
         copy.start()
         outs.append(copy)
+
+    for c in (0, 1):
+        combine(c)
+    forward(6)
+    combine(2)
+    forward(7)
+    for c in range(3, 8):
+        combine(c)
 
     for n in range(7):
         for s in (0, 1):

time: 63 us -> 64.2 us (1.019)
  the two profiles are of different devices: /device:TPU:8 before, /device:TPU:9 now
where the time goes in v6:
time: 64.2 us; the launch traced here: 64 us
  Pallas kernels  62.1 us (97%)
  local copies, waits for them, and re-layouts  1.88 us (3%)
    pallas_call x1, Pallas kernels, local(): pl.pallas_call(functools.partial(kernel, GX, GZ, PA, cells, NX, NZ), out_...  62.1 us
    unnamed x1, local copies, waits for them, and re-layouts  1.88 us

profile of v6, /device:TPU:9, one launch (start us, length us, event | category | flops | bytes accessed | tf_op | source)
XLA Modules:
  0.0 64.0 jit_solution(7000561546212794203)
XLA Ops:
  0.0 62.1 %shard_map.64 = f32[2,8,16,512]{3,2,1,0:T(8,128)} custom-call(s32[2]{0:T(128)} %spread.1, f32[2,8,16,512]{3,2,1,0:T(8,128)} %vel_hbm.1, f32[2,8,16,512]{3,2,1,0:T(8,128)} %now_hbm.1, f32[2,8,16,512]{3,2,1,0:T(8,128)} %prev_hbm.1, f32[8,16,512]{2,1,0:T(8,128)} %obs_hbm.1, s32[8,16,512]{2,1,0:T(8,128)} %rec_hbm.1), custom_call_target="tpu_custom_call" | custom-call | tf_op jit(solution)/shard_map/pallas_call | solution.py:487
  62.1 1.9 %copy.8 = f32[2,8,16,512]{3,2,1,0:T(8,128)} copy(f32[2,8,16,512]{3,2,1,0:T(8,128)} %shard_map.64) | data formatting | bytes 1048576
